TPU v7x, 32 devices: a whole 2x2x4 slice. The times are simulated.
32 devices in a mesh: groups: 2 (over y), blk: 4 (over z), win: 4 (over x, core).
Axes of the slice: x: 2, y: 2, z: 4, core: 2. Of those that a mesh axis runs over, the one named last changes fastest.
Arguments:
- spectra: bfloat16 [2, 24, 1024, 201], P(None, 'win', ('groups', 'blk')), parts along dimension 2
- channel_slot: int32 [1024], P(('groups', 'blk')), parts along dimension 0, may hold values from 0 to 511, as said below
- partners: int32 [2, 4], replicated, may hold values from 0 to 3, as said below
Outputs:
- correlations: bfloat16 [2, 1024, 101, 128], P(None, ('groups', 'blk', 'win')), parts along dimension 1
There are 2 independent parts, one for each index of `groups`. A program takes and returns all parts, laid end to end along the dimension named above; an argument that names none is the same for every part. Nothing has to cross between parts.
Inputs may be any that keep to these rules, and one draw needn't show every extreme that they name: channel_slot is a permutation of 0 to 511. For every acquisition shard s (channels s * 128 to s * 128 + 127) and every block b, exactly 32 of the shard's channels go to block b, and they take the slots b * 128 + s * 32 + q for q from 0 to 31. In round r, partners[r, i] = i XOR m_r for one value m_r of 1 to 3 per round; the rounds' values differ.
All inputs are finite; a program needn't handle non-finite values.
Results may differ from a plain program's by a relative error of at most 0.0057.
Values may be sent and summed in bfloat16 or wider, within the bound.
A program may use at most 128 MiB of HBM per device.

v0:
```python
import functools
import math

import jax
import jax.numpy as jnp
import numpy as np
from jax import lax
from jax.experimental import pallas as pl
from jax.experimental.pallas import tpu as pltpu
from jax.sharding import PartitionSpec as P

L = 101
ROUNDS = 2


eps_power = 1e-06
half_band = 2
tile_rows = 8


def whiten_into(piece, store, n_win, rows):
    power = None
    for win in range(n_win):
        value_array = piece(win).astype(jnp.float32)
        part = jnp.sum(value_array * value_array, axis=0)
        power = part if power is None else power + part
    nbins = power.shape[1]
    padding = jnp.zeros((power.shape[0], half_band), jnp.float32)
    padded = jnp.concatenate([padding, power, padding], axis=1)
    total = padded[:, 0:nbins]
    for offset in range(1, 2 * half_band + 1):
        total = total + padded[:, offset : offset + nbins]
    place = lax.broadcasted_iota(jnp.int32, power.shape, 1)
    count = 1 + jnp.minimum(place, half_band) + jnp.minimum(nbins - 1 - place, half_band)
    level = total / (count.astype(jnp.float32) * (n_win * rows // 2))
    scale = lax.rsqrt(level + eps_power)
    for win in range(n_win):
        store(win, (piece(win).astype(jnp.float32) * scale).astype(jnp.bfloat16))


def lag_table(nbins, nlags, windows):
    samples = 2 * (nbins - 1)
    freq = jnp.arange(nbins, dtype=jnp.int32)
    lags = jnp.arange(nlags, dtype=jnp.int32) - (nlags - 1) // 2
    phase_index = freq[:, None] * lags[None, :] % samples
    angle = 2.0 * math.pi / samples * phase_index.astype(jnp.float32)
    weight = jnp.where((freq == 0) | (freq == nbins - 1), 1.0, 2.0).astype(jnp.float32)
    norm = 1.0 / math.sqrt(windows * samples)
    cos_part = weight[:, None] * jnp.cos(angle) * norm
    sin_part = -weight[:, None] * jnp.sin(angle) * norm
    return jnp.concatenate([cos_part, sin_part], axis=0)


def correlate(both, right, table):
    cross = jnp.einsum(
        "cwak,wbk->kcab", both, right, preferred_element_type=jnp.float32
    ).astype(jnp.bfloat16)
    return jnp.einsum(
        "kcab,ckl->lab", cross, table, preferred_element_type=jnp.float32
    ).astype(jnp.bfloat16)


def flip(index, bit):
    return index + bit - 2 * bit * ((index // bit) % 2)


def exchange_kernel(
    n_blk, n_win, rounds, pair_ref, own_ref, *refs
):
    right_refs = refs[:rounds]
    both_ref, got_ref, src_ref, pair_send, pair_recv = refs[rounds : rounds + 5]
    pass_send, pass_recv, own_send, own_recv, local_sem = refs[rounds + 5 :]
    blk = lax.axis_index("blk")
    win = lax.axis_index("win")
    per_share = n_blk // n_win
    barrier = pltpu.get_barrier_semaphore()
    for step in range(1, n_blk * n_win):
        other = (blk * n_win + win + step) % (n_blk * n_win)
        pl.semaphore_signal(
            barrier,
            inc=1,
            device_id={"blk": other // n_win, "win": other % n_win},
            device_id_type=pl.DeviceIdType.MESH,
        )
    pl.semaphore_wait(barrier, n_blk * n_win - 1)

    def remote(src, dst, send, recv, to_blk, to_win):
        return pltpu.make_async_remote_copy(
            src_ref=src,
            dst_ref=dst,
            send_sem=send,
            recv_sem=recv,
            device_id={"blk": to_blk, "win": to_win},
            device_id_type=pl.DeviceIdType.MESH,
        )

    bits = []
    bit = n_win // 2
    while bit:
        bits.append(bit)
        bit //= 2

    order = list(range(n_blk))

    def across(step):
        other, each = blk, 1
        while each < n_blk:
            if step & each:
                other = flip(other, each)
            each *= 2
        return other

    def direct(step):
        dest = across(step)
        return remote(
            pair_ref.at[:, :, dest], got_ref.at[:, win, :, blk],
            pair_send.at[step], pair_recv.at[step], dest, win,
        )

    user = blk // per_share
    place = blk % per_share

    def own(step):
        dest = across(step)
        return remote(
            own_ref.at[:, dest], src_ref.at[win, :, place],
            own_send.at[step], own_recv.at[place * n_win + win], dest, user,
        )

    def passed(step, offset, over):
        origin = across(step)
        slot = win
        for each in bits:
            if offset & each:
                slot = flip(slot, each)
        target = got_ref.at[:, slot, :, origin]
        source = pair_ref.at[:, :, blk] if step == 0 and offset == 0 else target
        mark = (offset | over) - 1
        return remote(
            source, target, pass_send.at[mark, step], pass_recv.at[mark, step], blk, flip(win, over)
        )

    rows = pair_ref.shape[1]
    half = rows // 2
    keep = pltpu.make_async_copy(
        pair_ref.at[:, :, blk], got_ref.at[:, win, :, blk], local_sem.at[0]
    )
    keep.start()
    is_user = user == win

    def own_keep():
        return pltpu.make_async_copy(
            own_ref.at[:, blk], src_ref.at[win, :, place], local_sem.at[1]
        )

    @pl.when(is_user)
    def _():
        own_keep().start()

    passes = []
    held = [0]
    for over in bits:
        passes.extend((offset, over) for offset in held)
        held = held + [offset | over for offset in held]

    sends = []
    for offset, over in passes:
        if offset == 0:
            copy = passed(0, 0, over)
            copy.start()
            sends.append(copy)
    for step in order[1:]:
        copy = direct(step)
        copy.start()
        sends.append(copy)
    for step in order[1:]:
        copy = own(step)
        copy.start()
        sends.append(copy)

    @pl.when(jnp.logical_not(is_user))
    def _():
        own(0).start()

    keep.wait()

    @pl.when(is_user)
    def _():
        own_keep().wait()

    waited = set()

    def arrive(step, offset):
        if (step, offset) in waited:
            return
        waited.add((step, offset))
        if offset == 0:
            if step:
                direct(step).wait_recv()
        else:
            over = offset & -offset
            passed(step, offset - over, over).wait_recv()

    def finish(step):
        for offset in held:
            arrive(step, offset)
        origin = across(step)

        for index in range(rounds):

            def store(peer, white):
                right_refs[index][pl.ds(peer * rows, rows), origin] = white

            whiten_into(lambda peer: got_ref[index, peer, :, origin], store, n_win, rows)

    for turn in range(n_blk + 1):
        if 1 <= turn < n_blk:
            step = order[turn]
            arrive(step, 0)
            for offset, over in passes:
                if offset == 0:
                    copy = passed(step, 0, over)
                    copy.start()
                    sends.append(copy)
        if turn >= 1:
            step = order[turn - 1]
            for offset, over in passes:
                if offset:
                    arrive(step, offset)
                    copy = passed(step, offset, over)
                    copy.start()
                    sends.append(copy)
        if turn >= 2:
            finish(order[turn - 2])
    finish(order[n_blk - 1])
    for local in range(per_share):
        for peer in range(n_win):
            here = jnp.logical_and(blk == win * per_share + local, win == peer)

            @pl.when(jnp.logical_not(here))
            def _():
                piece = src_ref.at[peer, :, local]
                remote(
                    piece, piece, own_send.at[0], own_recv.at[local * n_win + peer], blk, win
                ).wait_recv()

    def one_shard(local, carry):
        def store(peer, white):
            both_ref[0, pl.ds(peer * rows, rows), local] = white
            both_ref[1, pl.ds(peer * rows, half), local] = white[half:]
            both_ref[1, pl.ds(peer * rows + half, half), local] = -white[:half]

        whiten_into(lambda peer: src_ref[peer, :, local], store, n_win, rows)
        return carry

    lax.fori_loop(0, per_share, one_shard, 0)

    for copy in sends:
        copy.wait_send()

    @pl.when(jnp.logical_not(is_user))
    def _():
        own(0).wait_send()


def exchange(pair, own, n_blk, n_win):
    rounds, rows, _, per_peer, nbins = pair.shape
    per_share = n_blk // n_win
    dtype = pair.dtype
    anywhere = pl.BlockSpec(memory_space=pl.ANY)
    vmem = pl.BlockSpec(memory_space=pltpu.VMEM)
    depth = n_win * rows
    return pl.pallas_call(
        functools.partial(exchange_kernel, n_blk, n_win, rounds),
        out_shape=(
            *[jax.ShapeDtypeStruct((depth, n_blk, per_peer, nbins), dtype)] * rounds,
            jax.ShapeDtypeStruct((2, depth, per_share, per_peer, nbins), dtype),
        ),
        in_specs=[anywhere, anywhere],
        out_specs=(vmem,) * (rounds + 1),
        scratch_shapes=[
            pltpu.VMEM((rounds, n_win, rows, n_blk, per_peer, nbins), dtype),
            pltpu.VMEM((n_win, rows, per_share, per_peer, nbins), dtype),
            pltpu.SemaphoreType.DMA((n_blk,)),
            pltpu.SemaphoreType.DMA((n_blk,)),
            pltpu.SemaphoreType.DMA((n_win - 1, n_blk)),
            pltpu.SemaphoreType.DMA((n_win - 1, n_blk)),
            pltpu.SemaphoreType.DMA((n_blk,)),
            pltpu.SemaphoreType.DMA((n_blk,)),
            pltpu.SemaphoreType.DMA((2,)),
        ],
        compiler_params=pltpu.CompilerParams(collective_id=0, has_side_effects=True),
    )(pair, own)


def plain_body(spectra, channel_slot, partners):
    n_blk = lax.axis_size("blk")
    n_win = lax.axis_size("win")
    parts, mine, chans, nbins = spectra.shape
    rows = parts * mine
    per_peer = chans // n_blk
    here = lax.axis_index("blk")
    share = chans // n_win
    windows = mine * n_win
    flat = spectra.reshape(rows, chans, nbins)
    wanted = jnp.concatenate([partners, jnp.arange(n_blk, dtype=jnp.int32)[None]], axis=0)
    slots = (
        wanted[:, :, None] * chans
        + here * per_peer
        + jnp.arange(per_peer, dtype=jnp.int32)[None, None, :]
    )
    selector = (slots[..., None] == channel_slot).astype(jnp.bfloat16)
    pair = jnp.einsum(
        "tzqc,xcf->txzqf", selector[:ROUNDS], flat, preferred_element_type=jnp.float32
    ).astype(jnp.bfloat16)
    own = jnp.einsum(
        "zqc,xcf->xzqf", selector[ROUNDS], flat, preferred_element_type=jnp.float32
    ).astype(jnp.bfloat16)
    *right, both = exchange(pair, own, n_blk, n_win)
    right = [each.reshape(n_win * rows, chans, nbins) for each in right]
    both = both.reshape(2, n_win * rows, share, nbins)
    table = lag_table(nbins, L, windows).reshape(2, nbins, L).astype(jnp.bfloat16)
    results = [correlate(both, right[index], table) for index in range(ROUNDS)]
    return jnp.stack(results, axis=0).transpose(0, 2, 1, 3)


def select_kernel(n_blk, slots_ref, partners_ref, x_ref, out_ref):
    dest = pl.program_id(0)
    here = lax.axis_index("blk")
    parts, _, nbins, chans = x_ref.shape
    kinds, groups = out_ref.shape[1], out_ref.shape[2]
    per_peer = chans // n_blk
    row = lax.broadcasted_iota(jnp.int32, (chans, chans), 0)
    slots = slots_ref[...]
    picks = []
    for kind in range(kinds):
        block = dest if kind == kinds - 1 else partners_ref[kind, dest]
        hit = slots == block * chans + here * per_peer + row % per_peer
        picks.append(
            jnp.concatenate(
                [
                    jnp.where(hit & (row // per_peer == y), 1.0, 0.0).astype(jnp.bfloat16)
                    for y in range(n_blk)
                ],
                axis=1,
            )
        )
    pick = jnp.concatenate(picks, axis=0)
    for group in range(groups):
        rows = [divmod(group * n_blk + y, parts) for y in range(n_blk)]
        wide = jnp.concatenate([x_ref[part, win] for win, part in rows], axis=1)
        got = lax.dot_general(
            wide, pick, (((1,), (1,)), ((), ())), preferred_element_type=jnp.float32
        ).astype(jnp.bfloat16)
        for kind in range(kinds):
            out_ref[0, kind, group] = got[:, kind * chans : (kind + 1) * chans]


def select(flat, slots, partners, n_blk, kinds):
    parts, mine, nbins, chans = flat.shape
    groups = parts * mine // n_blk
    return pl.pallas_call(
        functools.partial(select_kernel, n_blk),
        grid=(n_blk,),
        out_shape=jax.ShapeDtypeStruct((n_blk, kinds, groups, nbins, chans), flat.dtype),
        in_specs=[
            pl.BlockSpec((1, chans), lambda d: (0, 0)),
            pl.BlockSpec(memory_space=pltpu.SMEM),
            pl.BlockSpec(flat.shape, lambda d: (0, 0, 0, 0)),
        ],
        out_specs=pl.BlockSpec((1, kinds, groups, nbins, chans), lambda d: (d, 0, 0, 0, 0)),
    )(slots, partners, flat)


def across(index, step, count):
    other, bit = index, 1
    while bit < count:
        if step & bit:
            other = flip(other, bit)
        bit *= 2
    return other


def fused_kernel(
    n, rounds, ahead, unroll, piece_ref, regroup_ref, turn_ref, table_ref, out_ref,
    got_ref, own_ref, stage_ref, right_ref, left_ref, side_ref, cross_ref, lag_ref, pad_ref,
    scale_ref, far_send, far_recv, stage_send, stage_recv, pass_send, pass_recv,
    own_send, own_recv, local_sem,
):
    blk = lax.axis_index("blk")
    win = lax.axis_index("win")
    groups = piece_ref.shape[2]

    def remote(src, dst, send, recv, to_blk, to_win):
        return pltpu.make_async_remote_copy(
            src_ref=src,
            dst_ref=dst,
            send_sem=send,
            recv_sem=recv,
            device_id={"blk": to_blk, "win": to_win},
            device_id_type=pl.DeviceIdType.MESH,
        )

    barrier = pltpu.get_barrier_semaphore()
    for step in range(1, n):
        for to_blk, to_win in ((across(blk, step, n), win), (blk, across(win, step, n))):
            pl.semaphore_signal(
                barrier,
                inc=1,
                device_id={"blk": to_blk, "win": to_win},
                device_id_type=pl.DeviceIdType.MESH,
            )

    def far(turn, step, group):
        dest = across(blk, step, n)
        return remote(
            piece_ref.at[dest, turn, group], got_ref.at[turn, blk, win, group],
            far_send.at[turn, step, group], far_recv.at[turn, step, group], dest, win,
        )

    def staged(step, group):
        dest = across(blk, step, n)
        return remote(
            piece_ref.at[dest, rounds, group], stage_ref.at[blk, group],
            stage_send.at[step, group], stage_recv.at[blk, group], dest, win,
        )

    def own(step, group):
        user = across(win, step, n)
        return remote(
            stage_ref.at[user, group], own_ref.at[win, group],
            own_send.at[step, group], own_recv.at[step, group], blk, user,
        )

    bits = []
    bit = n // 2
    while bit:
        bits.append(bit)
        bit //= 2
    passes = []
    held = [0]
    for over in bits:
        passes.extend((offset, over) for offset in held)
        held = held + [offset | over for offset in held]

    def passed(turn, step, group, offset, over):
        origin = across(blk, step, n)
        piece = got_ref.at[turn, origin, across(win, offset, n), group]
        source = piece_ref.at[blk, turn, group] if step == 0 and offset == 0 else piece
        mark = (offset | over) - 1
        return remote(
            source, piece, pass_send.at[turn, step, group, mark],
            pass_recv.at[turn, step, group, mark], blk, flip(win, over),
        )

    sends = []

    def go(copy):
        copy.start()
        sends.append(copy)

    keeps = [
        pltpu.make_async_copy(
            piece_ref.at[blk, turn], got_ref.at[turn, blk, win], local_sem.at[turn]
        )
        for turn in range(rounds)
    ]
    homes = [
        pltpu.make_async_copy(
            piece_ref.at[blk, rounds, group], stage_ref.at[blk, group], stage_recv.at[blk, group]
        )
        for group in range(groups)
    ]
    for keep in homes + keeps:
        keep.start()
    pl.semaphore_wait(barrier, 2 * (n - 1))
    steps = list(range(n - 1, 0, -1))
    waves = [(None, group) for group in range(groups)]
    waves += [(turn, group) for turn in range(rounds) for group in range(groups)]

    def launch(index):
        if index < len(waves):
            turn, group = waves[index]
            for step in steps:
                go(staged(step, group) if turn is None else far(turn, step, group))

    for index in range(ahead):
        launch(index)
    for turn in range(rounds):
        for group in range(groups):
            for offset, over in passes:
                if offset == 0:
                    go(passed(turn, 0, group, 0, over))

    waited = set()

    def arrive(turn, step, group, offset):
        if (turn, step, group, offset) in waited:
            return
        waited.add((turn, step, group, offset))
        if offset == 0:
            if step:
                far(turn, step, group).wait_recv()
        else:
            over = offset & -offset
            passed(turn, step, group, offset - over, over).wait_recv()

    def onward(turn, step, group, first):
        for offset, over in passes:
            if (offset == 0) == first:
                arrive(turn, step, group, offset)
                go(passed(turn, step, group, offset, over))

    nbins, chans = piece_ref.shape[3:]
    per_peer = chans // n
    depth = n * groups * n
    stride = left_ref.shape[0] // depth
    both = 2 * per_peer
    apart = both + 1
    nlags = out_ref.shape[1]
    pad = (pad_ref.shape[0] - stride) // 2

    def level_scale(power):
        place = lax.broadcasted_iota(jnp.int32, (nbins, chans), 0)
        count = 1 + jnp.minimum(place, half_band) + jnp.minimum(nbins - 1 - place, half_band)
        pad_ref[pl.ds(pad, nbins)] = power
        near = pad_ref[pl.ds(pad - half_band, nbins)]
        for offset in range(1 - half_band, half_band + 1):
            near = near + pad_ref[pl.ds(pad + offset, nbins)]
        return lax.rsqrt(near / (count.astype(jnp.float32) * (depth // 2)) + eps_power)

    def own_scale():
        for group in range(groups):
            for step in range(1, n):
                own(step, group).wait_recv()
        for copy in mine:
            copy.wait()
        mine.clear()
        pad_ref[...] = jnp.zeros_like(pad_ref)
        scale_ref[...] = jnp.zeros_like(scale_ref)

        def add(index, total):
            value = own_ref[index // groups, index % groups].astype(jnp.float32)
            return total + value * value

        power = lax.fori_loop(0, n * groups, add, jnp.zeros((nbins, chans), jnp.float32))
        total = power
        for y in range(1, n):
            total = total + pltpu.roll(power, y * per_peer, 1)
        scale_ref[rounds] = level_scale(total)

    def own_left():
        def one(index, carry):
            value = own_ref[index // groups, index % groups].astype(jnp.float32)
            white = (value * scale_ref[rounds]).astype(jnp.bfloat16)
            wide = jnp.dot(white, turn_ref[...], preferred_element_type=jnp.float32)
            for y in range(n):
                left_ref[pl.ds((index * n + y) * stride, nbins)] = wide[
                    :, y * chans : (y + 1) * chans
                ]
            return carry

        lax.fori_loop(0, n * groups, one, 0)

    def binwise(one, share, shares):
        full = nbins // unroll
        low, high = full * share // shares, full * (share + 1) // shares

        def some(index, carry):
            for offset in range(unroll):
                one(index * unroll + offset)
            return carry

        lax.fori_loop(low, high, some, 0)
        if share == shares - 1:
            for bin_index in range(full * unroll, nbins):
                one(bin_index)

    def own_side(share, shares):
        def one(bin_index):
            side = left_ref[pl.ds(bin_index, depth, stride)].T
            side_ref[bin_index] = side[:both].astype(jnp.bfloat16)

        binwise(one, share, shares)

    def regroup(turn, group):
        for step in range(n):
            for offset in held:
                arrive(turn, step, group, offset)
        if group == 0:
            keeps[turn].wait()

        def one(slot, carry):
            raw = jnp.concatenate([got_ref[turn, shard, slot, group] for shard in range(n)], axis=1)
            wide = jnp.dot(raw, regroup_ref[...], preferred_element_type=jnp.float32)
            power = scale_ref[turn]
            for y in range(n):
                part = wide[:, y * chans : (y + 1) * chans]
                right_ref[turn, pl.ds(((slot * groups + group) * n + y) * stride, nbins)] = part
                power = power + part * part
            scale_ref[turn] = power
            return carry

        lax.fori_loop(0, n, one, 0)

    def right_scale(turn):
        scale_ref[turn] = level_scale(scale_ref[turn])

    def cross(turn, share, shares):
        def one(bin_index):
            right = right_ref[turn, pl.ds(bin_index, depth, stride)].astype(jnp.bfloat16)
            value = jnp.dot(side_ref[bin_index], right, preferred_element_type=jnp.float32)
            scale = scale_ref[turn, pl.ds(bin_index, 1)]
            value = jnp.where(scale > 0.0, value * scale, 0.0)
            cross_ref[turn, pl.ds(bin_index * apart, both)] = value

        binwise(one, share, shares)

    def to_lags(turn, share, shares):
        batch = math.gcd(per_peer // shares, 4)
        count = per_peer // shares // batch

        def some(index, carry):
            for offset in range(batch):
                source = batch * index + offset
                total = None
                for part in range(2):
                    rows = cross_ref[turn, pl.ds(part * per_peer + source, nbins, apart)]
                    term = jnp.dot(
                        table_ref[part], rows.astype(jnp.bfloat16), preferred_element_type=jnp.float32
                    )
                    total = term if total is None else total + term
                lag_ref[turn, pl.ds(source, nlags, per_peer + 1)] = total
            return carry

        lax.fori_loop(count * share, count * (share + 1), some, 0)

    def settle(turn):
        for lag in range(nlags):
            out_ref[turn, lag] = lag_ref[turn, pl.ds(lag * (per_peer + 1), per_peer)].astype(
                out_ref.dtype
            )

    tasks = [(groups, own_scale), (groups, own_left)]
    shares = 4
    for share in range(shares):
        tasks.append((groups, functools.partial(own_side, share, shares)))
    for turn in range(rounds):
        first = groups * (turn + 1) + 2
        for group in range(groups):
            tasks.append((first + group, functools.partial(regroup, turn, group)))
        first += groups - 1
        tasks.append((first, functools.partial(right_scale, turn)))
        shares = 4 if turn < rounds - 1 else 1
        for share in range(shares):
            tasks.append((first, functools.partial(cross, turn, share, shares)))
        for share in range(shares):
            tasks.append((first, functools.partial(to_lags, turn, share, shares)))
        tasks.append((first, functools.partial(settle, turn)))

    def tick(index):
        if tasks and tasks[0][0] <= index:
            tasks.pop(0)[1]()

    mine = []
    late = []
    for index, (turn, group) in enumerate(waves):
        if turn is None:
            for step in range(1, n):
                source = across(blk, step, n)
                piece = stage_ref.at[source, group]
                pltpu.make_async_copy(piece, piece, stage_recv.at[source, group]).wait()
            piece = stage_ref.at[blk, group]
            pltpu.make_async_copy(piece, piece, stage_recv.at[blk, group]).wait()
            for step in steps:
                go(own(step, group))
            copy = pltpu.make_async_copy(
                stage_ref.at[win, group], own_ref.at[win, group], local_sem.at[rounds + group]
            )
            copy.start()
            mine.append(copy)
        else:
            for step in range(1, n):
                onward(turn, step, group, True)
        launch(index + ahead)
        for item in late:
            onward(*item, False)
        if turn is not None:
            for _ in range(3):
                tick(index)
        if turn is None:
            late = [(turn, 0, group) for turn in range(rounds)]
        else:
            late = [(turn, step, group) for step in range(1, n)]
    for item in late:
        onward(*item, False)
    while tasks:
        tasks.pop(0)[1]()
    for copy in sends:
        copy.wait_send()


def fused(pieces, n, rounds, windows):
    shape, dtype = pieces.shape[2:], pieces.dtype
    groups, nbins, chans = shape
    per_peer = chans // n
    depth = n * groups * n
    stride = (nbins + 7) // 8 * 8
    wide, turned = lane_spread(n, per_peer, chans)
    table = fixed_table(nbins, L, windows)
    vmem = pl.BlockSpec(memory_space=pltpu.VMEM)
    dma = pltpu.SemaphoreType.DMA
    return pl.pallas_call(
        functools.partial(fused_kernel, n, rounds, 2, 16),
        out_shape=jax.ShapeDtypeStruct((rounds, L, per_peer, chans), jnp.bfloat16),
        in_specs=[vmem] * 4,
        out_specs=vmem,
        scratch_shapes=[
            pltpu.VMEM((rounds, n, n, *shape), dtype),
            pltpu.VMEM((n, *shape), dtype),
            pltpu.VMEM((n, *shape), dtype),
            pltpu.VMEM((rounds, depth * stride, chans), jnp.float32),
            pltpu.VMEM((depth * stride, chans), jnp.float32),
            pltpu.VMEM((nbins, 2 * per_peer, depth), jnp.bfloat16),
            pltpu.VMEM((rounds, nbins * (2 * per_peer + 1), chans), jnp.float32),
            pltpu.VMEM((rounds, L * (per_peer + 1), chans), jnp.float32),
            pltpu.VMEM((stride + 16, chans), jnp.float32),
            pltpu.VMEM((rounds + 1, nbins, chans), jnp.float32),
            dma((rounds, n, groups)), dma((rounds, n, groups)), dma((n, groups)), dma((n, groups)),
            dma((rounds, n, groups, n - 1)), dma((rounds, n, groups, n - 1)),
            dma((n, groups)), dma((n, groups)), dma((rounds + groups,)),
        ],
        compiler_params=pltpu.CompilerParams(
            collective_id=1, has_side_effects=True, vmem_limit_bytes=48 * 2**20
        ),
    )(
        pieces, jnp.asarray(wide, jnp.bfloat16), jnp.asarray(turned, jnp.bfloat16),
        jnp.asarray(table, jnp.bfloat16),
    )


def lane_spread(n, per_peer, chans):
    regroup = np.zeros((n, n, per_peer, n, n, per_peer), np.float32)
    for shard in range(n):
        for y in range(n):
            for q in range(per_peer):
                regroup[shard, y, q, y, shard, q] = 1.0
    turned = np.zeros((n, per_peer, n, chans), np.float32)
    for y in range(n):
        for q in range(per_peer):
            turned[y, q, y, q] = 1.0
            part = y % 2
            turned[y + 1 - 2 * part, q, y, per_peer + q] = 1.0 if part == 0 else -1.0
    return regroup.reshape(n * chans, n * chans), turned.reshape(chans, n * chans)


def fixed_table(nbins, nlags, windows):
    samples = 2 * (nbins - 1)
    freq = np.arange(nbins)
    lags = np.arange(nlags) - (nlags - 1) // 2
    angle = 2.0 * np.pi / samples * (lags[:, None] * freq[None, :] % samples)
    weight = np.where((freq == 0) | (freq == nbins - 1), 1.0, 2.0) / np.sqrt(windows * samples)
    return np.stack([np.cos(angle) * weight, -np.sin(angle) * weight]).astype(np.float32)


def dense_body(spectra, channel_slot, partners):
    n = lax.axis_size("blk")
    parts, mine, chans, nbins = spectra.shape
    rounds = partners.shape[0]
    flat = spectra.transpose(0, 1, 3, 2)
    pieces = select(flat, channel_slot.reshape(1, chans), partners, n, rounds + 1)
    return fused(pieces, n, rounds, mine * n).transpose(0, 2, 1, 3)


def body(spectra, channel_slot, partners):
    n_blk = lax.axis_size("blk")
    rows = spectra.shape[0] * spectra.shape[1]
    fits = n_blk == lax.axis_size("win") and rows % n_blk == 0 and n_blk % spectra.shape[0] == 0
    if fits and 2 * spectra.shape[2] // n_blk <= spectra.shape[2]:
        return dense_body(spectra, channel_slot, partners)
    return plain_body(spectra, channel_slot, partners)


def solution(mesh):
    in_specs = (P(None, "win", ("groups", "blk"), None), P(("groups", "blk")), P())
    out_specs = P(None, ("groups", "blk", "win"), None, None)
    return jax.shard_map(body, mesh=mesh, in_specs=in_specs, out_specs=out_specs, check_vma=False)
```

profile of v0, /device:TPU:0, one launch (start us, length us, event | category | flops | bytes accessed | tf_op | source)
XLA Modules:
  0.0 75.0 jit_solution(2919445652471355124)
XLA Ops:
  0.0 0.0 copy-start.1
  0.0 0.0 copy-start.2
  0.0 0.0 copy-start.3
  0.0 2.1 %copy.9 = bf16[2,6,128,201]{2,3,1,0:T(8,128)(2,1)} copy(bf16[2,6,128,201]{2,0,3,1:T(2,128)(2,1)} %param.6) | data formatting | bytes 1234944 | tf_op args[0]
  2.1 4.3 %shard_map.64.piece_ref = bf16[4,3,3,201,128]{4,3,2,1,0:T(8,128)(2,1)} custom-call(s32[1,128]{1,0:T(1,128)} %bitcast.7, s32[2,4]{1,0:T(2,128)} %partners_ref.1, bf16[2,6,201,128]{3,2,1,0:T(8,128)(2,1)} %bitcast.6), custom_call_target="tpu_custom_call" | custom-call | tf_op jit(solution)/shard_map/pallas_call | solution.py:362
  6.3 0.0 copy-done.1
  6.3 0.0 copy-done.2
  6.3 0.0 copy-done.3
  6.3 0.0 copy-start
  6.3 1.5 %copy-done = bf16[4,3,3,201,128]{4,3,2,1,0:T(8,128)(2,1)S(1)} copy-done((bf16[4,3,3,201,128]{4,3,2,1,0:T(8,128)(2,1)S(1)}, bf16[4,3,3,201,128]{4,3,2,1,0:T(8,128)(2,1)}, u32[]{:S(2)}) %copy-start) | copy-done | bytes 1852440
  7.9 65.9 %shard_map.65 = bf16[2,101,32,128]{3,2,1,0:T(8,128)(2,1)S(1)} custom-call(bf16[4,3,3,201,128]{4,3,2,1,0:T(8,128)(2,1)S(1)} %copy-done, bf16[512,512]{1,0:T(8,128)(2,1)S(1)} %copy-done.1, bf16[128,512]{1,0:T(8,128)(2,1)S(1)} %copy-done.2, bf16[2,101,201]{2,1,0:T(8,128)(2,1)S(1)} %copy-done.3), custom_call_target="tpu_custom_call" | custom-call | tf_op jit(solution)/shard_map/pallas_call | solution.py:713
  73.8 1.2 %copy.11 = bf16[2,32,101,128]{3,1,2,0:T(8,128)(2,1)} copy(bf16[2,32,101,128]{3,1,2,0:T(8,128)(2,1)S(1)} %bitcast.5) | data formatting | bytes 3309568
Async XLA Ops:
  0.0 6.3 %copy-start.1 = (bf16[512,512]{1,0:T(8,128)(2,1)S(1)}, bf16[512,512]{1,0:T(8,128)(2,1)}, u32[]{:S(2)}) copy-start(bf16[512,512]{1,0:T(8,128)(2,1)} %constant.6.clone.regroup_ref) | copy-start | bytes 1572868
  0.0 6.3 %copy-start.2 = (bf16[128,512]{1,0:T(8,128)(2,1)S(1)}, bf16[128,512]{1,0:T(8,128)(2,1)}, u32[]{:S(2)}) copy-start(bf16[128,512]{1,0:T(8,128)(2,1)} %constant.7.clone.turn_ref) | copy-start | bytes 393220
  0.0 6.3 %copy-start.3 = (bf16[2,101,201]{2,1,0:T(8,128)(2,1)S(1)}, bf16[2,101,201]{2,1,0:T(8,128)(2,1)}, u32[]{:S(2)}) copy-start(bf16[2,101,201]{2,1,0:T(8,128)(2,1)} %constant.8.clone.table_ref) | copy-start | bytes 243616
  6.3 1.5 %copy-start = (bf16[4,3,3,201,128]{4,3,2,1,0:T(8,128)(2,1)S(1)}, bf16[4,3,3,201,128]{4,3,2,1,0:T(8,128)(2,1)}, u32[]{:S(2)}) copy-start(bf16[4,3,3,201,128]{4,3,2,1,0:T(8,128)(2,1)} %shard_map.64.piece_ref) | copy-start | bytes 5557252
where the time goes:
time: 75.1 us; the launch traced here: 75 us
  Pallas kernels  70.2 us (93%)
  local copies, waits for them, and re-layouts  4.76 us (6%)
    pallas_call x1, Pallas kernels, fused(): pl.pallas_call(functools.partial(fused_kernel, n, rounds, 2, 16), out_sha...  65.9 us
    unnamed x10, local copies, waits for them, and re-layouts  4.76 us
    pallas_call x1, Pallas kernels, select(): pl.pallas_call(functools.partial(select_kernel, n_blk), grid=(n_blk,), ou...  4.26 us

commit v1 on v0

--- a/solution.py
+++ b/solution.py
@@ -617,7 +617,7 @@
         binwise(one, share, shares)
 
     def to_lags(turn, share, shares):
-        batch = math.gcd(per_peer // shares, 4)
+        batch = math.gcd(per_peer // shares, 8)
         count = per_peer // shares // batch
 
         def some(index, carry):

time: 75.1 us -> 73.3 us (0.976)
  Pallas kernels: 70.2 us -> 68.3 us
    pallas_call x1, Pallas kernels: 65.9 us -> 64 us  [fused(): pl.pallas_call(functools.partial(fused_kernel, n, rounds, 2, 16), out_sha...]
where the time goes in v1:
time: 73.3 us; the launch traced here: 73.1 us
  Pallas kernels  68.3 us (93%)
  local copies, waits for them, and re-layouts  4.76 us (6%)
    pallas_call x1, Pallas kernels, fused(): pl.pallas_call(functools.partial(fused_kernel, n, rounds, 2, 16), out_sha...  64 us
    unnamed x10, local copies, waits for them, and re-layouts  4.76 us
    pallas_call x1, Pallas kernels, select(): pl.pallas_call(functools.partial(select_kernel, n_blk), grid=(n_blk,), ou...  4.26 us

profile of v1, /device:TPU:0, one launch (start us, length us, event | category | flops | bytes accessed | tf_op | source)
XLA Modules:
  0.0 73.1 jit_solution(12565953352769309264)
XLA Ops:
  0.0 0.0 copy-start.1
  0.0 0.0 copy-start.2
  0.0 0.0 copy-start.3
  0.0 2.1 %copy.9 = bf16[2,6,128,201]{2,3,1,0:T(8,128)(2,1)} copy(bf16[2,6,128,201]{2,0,3,1:T(2,128)(2,1)} %param.6) | data formatting | bytes 1234944 | tf_op args[0]
  2.1 4.3 %shard_map.64.piece_ref = bf16[4,3,3,201,128]{4,3,2,1,0:T(8,128)(2,1)} custom-call(s32[1,128]{1,0:T(1,128)} %bitcast.7, s32[2,4]{1,0:T(2,128)} %partners_ref.1, bf16[2,6,201,128]{3,2,1,0:T(8,128)(2,1)} %bitcast.6), custom_call_target="tpu_custom_call" | custom-call | tf_op jit(solution)/shard_map/pallas_call | solution.py:362
  6.3 0.0 copy-done.1
  6.3 0.0 copy-done.2
  6.3 0.0 copy-done.3
  6.3 0.0 copy-start
  6.3 1.5 %copy-done = bf16[4,3,3,201,128]{4,3,2,1,0:T(8,128)(2,1)S(1)} copy-done((bf16[4,3,3,201,128]{4,3,2,1,0:T(8,128)(2,1)S(1)}, bf16[4,3,3,201,128]{4,3,2,1,0:T(8,128)(2,1)}, u32[]{:S(2)}) %copy-start) | copy-done | bytes 1852440
  7.9 64.0 %shard_map.65 = bf16[2,101,32,128]{3,2,1,0:T(8,128)(2,1)S(1)} custom-call(bf16[4,3,3,201,128]{4,3,2,1,0:T(8,128)(2,1)S(1)} %copy-done, bf16[512,512]{1,0:T(8,128)(2,1)S(1)} %copy-done.1, bf16[128,512]{1,0:T(8,128)(2,1)S(1)} %copy-done.2, bf16[2,101,201]{2,1,0:T(8,128)(2,1)S(1)} %copy-done.3), custom_call_target="tpu_custom_call" | custom-call | tf_op jit(solution)/shard_map/pallas_call | solution.py:713
  71.9 1.2 %copy.11 = bf16[2,32,101,128]{3,1,2,0:T(8,128)(2,1)} copy(bf16[2,32,101,128]{3,1,2,0:T(8,128)(2,1)S(1)} %bitcast.5) | data formatting | bytes 3309568
Async XLA Ops:
  0.0 6.3 %copy-start.1 = (bf16[512,512]{1,0:T(8,128)(2,1)S(1)}, bf16[512,512]{1,0:T(8,128)(2,1)}, u32[]{:S(2)}) copy-start(bf16[512,512]{1,0:T(8,128)(2,1)} %constant.6.clone.regroup_ref) | copy-start | bytes 1572868
  0.0 6.3 %copy-start.2 = (bf16[128,512]{1,0:T(8,128)(2,1)S(1)}, bf16[128,512]{1,0:T(8,128)(2,1)}, u32[]{:S(2)}) copy-start(bf16[128,512]{1,0:T(8,128)(2,1)} %constant.7.clone.turn_ref) | copy-start | bytes 393220
  0.0 6.3 %copy-start.3 = (bf16[2,101,201]{2,1,0:T(8,128)(2,1)S(1)}, bf16[2,101,201]{2,1,0:T(8,128)(2,1)}, u32[]{:S(2)}) copy-start(bf16[2,101,201]{2,1,0:T(8,128)(2,1)} %constant.8.clone.table_ref) | copy-start | bytes 243616
  6.3 1.5 %copy-start = (bf16[4,3,3,201,128]{4,3,2,1,0:T(8,128)(2,1)S(1)}, bf16[4,3,3,201,128]{4,3,2,1,0:T(8,128)(2,1)}, u32[]{:S(2)}) copy-start(bf16[4,3,3,201,128]{4,3,2,1,0:T(8,128)(2,1)} %shard_map.64.piece_ref) | copy-start | bytes 5557252
